TPU v7x, 32 devices: a whole 2x2x4 slice. The times are simulated.
32 devices in a mesh: cuts: 2 (over y), idx: 8 (over z, x), half: 2 (over core).
Axes of the slice: x: 2, y: 2, z: 4, core: 2. Of those that a mesh axis runs over, the one named last changes fastest.
Arguments:
- left_factor: float32 [2, 4, 64, 1024, 256], P('half', 'cuts', 'idx'), parts along dimension 1, may hold values from -6 to 6
- right_factor: float32 [2, 4, 64, 256, 1024], P('half', 'cuts', None, 'idx'), parts along dimension 1, may hold values from -0.25 to 0.25
Outputs:
- amplitudes: float32 [1024, 4, 1024], P(('idx', 'half'), 'cuts'), parts along dimension 1
There are 2 independent parts, one for each index of `cuts`. A program takes and returns all parts, laid end to end along the dimension named above; each array names one. Nothing has to cross between parts.
All inputs are finite; a program needn't handle non-finite values.
Results may differ from a plain program's by a relative error of at most 0.0003.
Values sent between devices are 32-bit elements; how exact they have to be, the bound alone decides.
A program may use at most 256 MiB of HBM per device.

v0:
```python
import math
import jax
import jax.numpy as jnp
from jax import lax
from jax.sharding import PartitionSpec as P

HIGH = lax.Precision.HIGH
CHUNKS = (3, 1)


def swapped(x, axis, bit):
    return lax.ppermute(x, axis, [(i, i ^ 1 << bit) for i in range(lax.axis_size(axis))])


def complex_product(left_real, left_imag, right_real, right_imag, pattern):
    first_term = jnp.einsum(pattern, left_real, right_real, precision=HIGH)
    second_term = jnp.einsum(pattern, left_imag, right_imag, precision=HIGH)
    mixed_term = jnp.einsum(pattern, left_real + left_imag, right_real + right_imag, precision=HIGH)
    return (first_term - second_term, mixed_term - first_term - second_term)


def by_columns(left_local, right_local, norm_scale):
    columns = lax.all_to_all(right_local, "idx", split_axis=1, concat_axis=2, tiled=True)
    merged = jnp.stack(
        complex_product(left_local[0], left_local[1], columns[0], columns[1], "bmk,bkn->bmn")
    )
    half_cols = merged.shape[3] // 2
    half_index = lax.axis_index("half")
    outgoing = lax.dynamic_slice_in_dim(merged, (1 - half_index) * half_cols, half_cols, 3)
    own_slab = lax.dynamic_slice_in_dim(merged, half_index * half_cols, half_cols, 3)
    other_slab = swapped(outgoing, "half", 0)
    is_lower = half_index == 0
    first_pair = jnp.where(is_lower, own_slab, other_slab)
    second_pair = jnp.where(is_lower, other_slab, own_slab)
    real_part, imag_part = complex_product(
        first_pair[0], first_pair[1], second_pair[0], second_pair[1], "bmn,bon->mo"
    )
    return jnp.stack([real_part, imag_part], axis=1) * norm_scale


def by_batch(left_local, right_local, norm_scale):
    idx, half = (lax.axis_size("idx"), lax.axis_size("half"))
    planes, batch, rows, between = right_local.shape
    mine = left_local.shape[1] // half
    half_index = lax.axis_index("half")
    blocks = right_local.reshape(planes, idx * half, mine, rows, between)
    sizes = CHUNKS if sum(CHUNKS) == mine else (mine,)
    received = []
    start = 0
    for size in sizes:
        piece = blocks[:, :, start : start + size].transpose(1, 0, 2, 3, 4)
        received.append(
            lax.all_to_all(piece, ("idx", "half"), split_axis=0, concat_axis=0, tiled=True)
        )
        start += size
    outgoing = lax.dynamic_slice_in_dim(left_local, (1 - half_index) * mine, mine, 1)
    own = lax.dynamic_slice_in_dim(left_local, half_index * mine, mine, 1)
    other = swapped(outgoing, "half", 0)
    is_lower = half_index == 0
    first = jnp.where(is_lower, own, other)
    second = jnp.where(is_lower, other, own)
    total = None
    start = 0
    for size, got in zip(sizes, received):
        got = got.reshape(idx, half, planes, size, rows, between)
        pairs = got.transpose(1, 2, 3, 0, 4, 5).reshape(half, planes, size, idx * rows, between)
        inner = complex_product(pairs[0, 0], pairs[0, 1], pairs[1, 0], pairs[1, 1], "bkn,bln->bkl")
        a = first[:, start : start + size]
        b = second[:, start : start + size]
        partial = complex_product(a[0], a[1], inner[0], inner[1], "bmk,bkl->bml")
        term = complex_product(partial[0], partial[1], b[0], b[1], "bml,bol->mo")
        total = term if total is None else (total[0] + term[0], total[1] + term[1])
        start += size
    return jnp.stack(total, axis=1) * norm_scale


def on_device(left_factor, right_factor):
    left_local = left_factor[0]
    right_local = right_factor[0]
    batch, between = (right_local.shape[1], right_local.shape[3])
    norm_scale = 1.0 / math.sqrt(2.0 * batch * between)
    shared = left_local.shape[1] % lax.axis_size("half") == 0
    form = by_batch if shared else by_columns
    return lax.psum_scatter(
        form(left_local, right_local, norm_scale), ("idx", "half"), scatter_dimension=0, tiled=True
    )


def solution(mesh):
    return jax.shard_map(
        on_device,
        mesh=mesh,
        in_specs=(P("half", "cuts", "idx", None, None), P("half", "cuts", None, "idx", None)),
        out_specs=P(("idx", "half"), "cuts", None),
        check_vma=False,
    )
```

profile of v0, /device:TPU:0, one launch (start us, length us, event | category | flops | bytes accessed | tf_op | source)
XLA Modules:
  0.0 577.8 jit_solution(6922426632892912840)
XLA Ops:
  6.5 2.5 slice_bitcast_fusion.1
  9.0 2.3 copy.17
  11.3 7.4 %all-to-all-start.1 = ((f32[16,2,1,32,1024]{4,3,2,1,0:T(8,128)}), f32[16,2,1,32,1024]{4,3,2,1,0:T(8,128)}, u32[]{:S(2)}, u32[]{:S(2)}) async-start(f32[16,2,1,32,1024]{4,3,2,1,0:T(8,128)} %copy.17), calls=%async_computation.1 | async-start | bytes 8388608 | tf_op jit(solution)/shard_map/all_to_all | solution.py:53
  18.8 11.8 %slice_bitcast_fusion = f32[16,2,3,32,1024]{4,3,2,0,1:T(8,128)} fusion(f32[2,16,4,32,1024]{4,3,2,1,0:T(8,128)} %bitcast.163), kind=kLoop, calls=%fused_computation | loop fusion | bytes 25165824 | tf_op jit(solution)/shard_map/transpose | solution.py:51
  30.6 11.8 %copy.15 = f32[16,2,3,32,1024]{4,3,2,1,0:T(8,128)} copy(f32[16,2,3,32,1024]{4,3,2,0,1:T(8,128)} %slice_bitcast_fusion) | data formatting | bytes 25165824 | tf_op jit(solution)/shard_map/transpose | solution.py:51
  42.4 53.9 %all-to-all-done.1 = f32[16,2,1,32,1024]{4,3,2,1,0:T(8,128)} async-done(((f32[16,2,1,32,1024]{4,3,2,1,0:T(8,128)}), f32[16,2,1,32,1024]{4,3,2,1,0:T(8,128)}, u32[]{:S(2)}, u32[]{:S(2)}) %all-to-all-start.1) | async-done | bytes 4194336 | tf_op jit(solution)/shard_map/all_to_all | solution.py:53
  96.3 19.7 %all-to-all-start = ((f32[16,2,3,32,1024]{4,3,2,1,0:T(8,128)}), f32[16,2,3,32,1024]{4,3,2,1,0:T(8,128)}, u32[]{:S(2)}, u32[]{:S(2)}) async-start(f32[16,2,3,32,1024]{4,3,2,1,0:T(8,128)} %copy.15), calls=%async_computation | async-start | bytes 25165824 | tf_op jit(solution)/shard_map/all_to_all | solution.py:53
  116.1 7.2 %dynamic-slice_bitcast_fusion = f32[2,4,1024,256]{3,2,1,0:T(8,128)} fusion(f32[1,2,8,1024,256]{4,3,2,1,0:T(8,128)} %param.2, s32[]{:T(128)S(6)} %select_n.20), kind=kLoop, calls=%fused_computation.4 | loop fusion | bytes 16777220 | tf_op jit(solution)/shard_map/dynamic_slice | solution.py:56
  123.6 2.5 copy.18
  126.1 0.6 fusion.50
  127.3 0.7 fusion.38
  128.0 8.7 %collective-permute-done = f32[2,4,1024,256]{3,2,1,0:T(8,128)} collective-permute-done((f32[2,4,1024,256]{3,2,1,0:T(8,128)}, f32[2,4,1024,256]{3,2,1,0:T(8,128)}, u32[]{:S(2)}, u32[]{:S(2)}) %collective-permute-start) | collective-permute-done | bytes 8388640 | tf_op jit(solution)/shard_map/ppermute | solution.py:12
  136.7 7.0 %bitcast_select_fusion = (f32[2,4,1024,256]{3,2,1,0:T(8,128)S(1)}, f32[2,4,1024,256]{3,2,1,0:T(8,128)S(1)}) fusion(f32[2,4,1024,256]{3,2,1,0:T(8,128)} %collective-permute-done, f32[1,2,8,1024,256]{4,3,2,1,0:T(8,128)} %param.2, s32[]{:T(128)S(6)} %select_n.19, pred[]{:T(512)S(6)} %eq.3), kind=kLoop, calls=%fused_computation.2 | loop fusion | flops 4194304 | bytes 33554436 | tf_op jit(solution)/shard_map/jit(_where)/select_n | solution.py:61
  145.6 1.4 copy-done.1
  147.0 3.8 fusion.41
  150.8 3.9 fusion.44
  154.7 3.8 fusion.39
  158.5 181.1 %all-to-all-done = f32[16,2,3,32,1024]{4,3,2,1,0:T(8,128)} async-done(((f32[16,2,3,32,1024]{4,3,2,1,0:T(8,128)}), f32[16,2,3,32,1024]{4,3,2,1,0:T(8,128)}, u32[]{:S(2)}, u32[]{:S(2)}) %all-to-all-start) | async-done | bytes 12582944 | tf_op jit(solution)/shard_map/all_to_all | solution.py:53
  339.6 11.8 %copy.16 = f32[2,2,3,8,32,1024]{5,4,3,2,1,0:T(8,128)} copy(f32[2,2,3,8,32,1024]{5,4,2,1,0,3:T(8,128)} %bitcast.6) | data formatting | bytes 25165824 | tf_op jit(solution)/shard_map/transpose | solution.py:66
  351.5 4.6 fusion.15
  356.0 5.4 fusion.14
  361.4 1.8 fusion.33
  363.2 3.4 fusion.13
  366.7 1.5 fusion.16
  368.2 3.5 subtract_subtract_fusion
  371.7 6.9 %fusion.17 = f32[1024,1024,1]{1,0,2:T(8,128)} fusion(f32[2,4,1024,256]{3,2,1,0:T(8,128)S(1)} %bitcast.158, f32[3,1024,256]{2,1,0:T(8,128)S(1)} %fusion.13, f32[3,1024,256]{2,1,0:T(8,128)S(1)} %fusion.16), kind=kOutput, calls=%fused_computation.34 | convolution fusion | flops 4832624640 | bytes 13631488 | tf_op jit(solution)/shard_map/bml,bol->mo/dot_general | solution.py:16
  378.6 6.9 %fusion.18 = f32[1024,1024,1]{1,0,2:T(8,128)} fusion(f32[3,1024,256]{2,1,0:T(8,128)S(1)} %copy-done.4, f32[2,4,1024,256]{3,2,1,0:T(8,128)S(1)} %bitcast.158), kind=kOutput, calls=%fused_computation.35 | convolution fusion | flops 4831838208 | bytes 10485760 | tf_op jit(solution)/shard_map/bml,bol->mo/dot_general | solution.py:17
  385.5 8.7 %fusion.4 = f32[1024,1,1024]{2,0,1:T(8,128)} fusion(f32[1024,1024,1]{1,0,2:T(8,128)} %fusion.18, f32[1024,1024,1]{1,0,2:T(8,128)} %fusion.17, f32[1024,1024]{1,0:T(8,128)S(1)} %copy-done.3, f32[1024,1024]{1,0:T(8,128)} %fusion.41), kind=kLoop, calls=%fused_computation.12 | loop fusion | flops 3145728 | bytes 20971520 | tf_op jit(solution)/shard_map/stack | solution.py:74
  394.2 13.3 %fusion.2 = f32[1024,1,1024]{2,0,1:T(8,128)} fusion(f32[1024,1024,1]{1,0,2:T(8,128)} %fusion.18, f32[1024,1024,1]{1,0,2:T(8,128)} %fusion.17, f32[1024,1024]{1,0:T(8,128)} %fusion.41, f32[1024,1024]{1,0:T(8,128)} %fusion.39, f32[1024,1024]{1,0:T(8,128)S(1)} %copy-done.3, f32[2,4,1024,256]{3,2,1,0:T(8,128)} %copy-done.2, ...), kind=kOutput, calls=%fused_computation.9 | convolution fusion | flops 4839440384 | bytes 40894464 | tf_op jit(solution)/shard_map/bml,bol->mo/dot_general | solution.py:18
  407.5 8.7 %maximum_multiply_fusion = f32[1024,2,1024]{2,0,1:T(8,128)} fusion(f32[1024,1,1024]{2,0,1:T(8,128)} %fusion.2, f32[1024,1,1024]{2,0,1:T(8,128)} %fusion.4), kind=kLoop, calls=%fused_computation.1 | loop fusion | flops 4194304 | bytes 16777216 | tf_op jit(solution)/shard_map/mul | solution.py:74
  416.2 152.3 %reduce-scatter.2.cloned.1.call-done = f32[64,2,1024]{2,0,1:T(8,128)} async-done(((f32[1024,2,1024]{2,0,1:T(8,128)}), f32[64,2,1024]{2,0,1:T(8,128)}) %reduce-scatter.2.cloned.1.call-update) | async-done | bytes 524304 | tf_op jit(solution)/shard_map/reduce_scatter | solution.py:84
  568.5 2.2 copy.19
  (26 shorter events, 2.8 us)
Async XLA Ops:
  11.3 85.0 %all-to-all-start.1 = ((f32[16,2,1,32,1024]{4,3,2,1,0:T(8,128)}), f32[16,2,1,32,1024]{4,3,2,1,0:T(8,128)}, u32[]{:S(2)}, u32[]{:S(2)}) async-start(f32[16,2,1,32,1024]{4,3,2,1,0:T(8,128)} %copy.17), calls=%async_computation.1 | async-start | bytes 8388608 | tf_op jit(solution)/shard_map/all_to_all | solution.py:53
  96.3 243.3 %all-to-all-start = ((f32[16,2,3,32,1024]{4,3,2,1,0:T(8,128)}), f32[16,2,3,32,1024]{4,3,2,1,0:T(8,128)}, u32[]{:S(2)}, u32[]{:S(2)}) async-start(f32[16,2,3,32,1024]{4,3,2,1,0:T(8,128)} %copy.15), calls=%async_computation | async-start | bytes 25165824 | tf_op jit(solution)/shard_map/all_to_all | solution.py:53
  116.0 452.5 %reduce-scatter.2.cloned.1.call-start = ((), (), s32[]{:S(2)}) async-start(), calls=%async_computation.3 | async-start | bytes 8912896 | tf_op jit(solution)/shard_map/reduce_scatter | solution.py:84
  123.2 13.5 %collective-permute-start = (f32[2,4,1024,256]{3,2,1,0:T(8,128)}, f32[2,4,1024,256]{3,2,1,0:T(8,128)}, u32[]{:S(2)}, u32[]{:S(2)}) collective-permute-start(f32[2,4,1024,256]{3,2,1,0:T(8,128)} %dynamic-slice_bitcast_fusion), channel_id=1, source_target_pairs={{0,1},{1,0},{2,3},{3,2},{4,5},{5,4},{6,7},{7,6},{8,9},{9,8},{10,11... | collective-permute-start | bytes 25165832 | tf_op jit(solution)/shard_map/ppermute | solution.py:12
  143.7 3.2 copy-start.1
  143.8 10.9 %copy-start.2 = (f32[2,4,1024,256]{3,2,1,0:T(8,128)}, f32[2,4,1024,256]{3,2,1,0:T(8,128)S(1)}, u32[]{:S(2)}) copy-start(f32[2,4,1024,256]{3,2,1,0:T(8,128)S(1)} %get-tuple-element.5) | copy-start | bytes 25165828
  351.5 9.9 %copy-start = (f32[2,2,3,8,32,1024]{5,4,3,2,1,0:T(8,128)S(1)}, f32[2,2,3,8,32,1024]{5,4,3,2,1,0:T(8,128)}, u32[]{:S(2)}) copy-start(f32[2,2,3,8,32,1024]{5,4,3,2,1,0:T(8,128)} %copy.16) | copy-start | bytes 37748740
  356.0 10.6 %slice-start = ((s8[8388608]{0:T(1024)(128)(4,1)}), s8[4194304]{0:T(1024)(128)(4,1)S(1)}, s32[]{:S(2)}) async-start(s8[8388608]{0:T(1024)(128)(4,1)} %bitcast.155), calls=%async_computation.4 | async-start | bytes 8388608
  361.4 5.2 slice-start.1
  366.7 5.1 slice-start.2
  368.2 3.5 slice-start.3
  371.7 6.9 %copy-start.4 = (f32[3,1024,256]{2,1,0:T(8,128)S(1)}, f32[3,1024,256]{2,1,0:T(8,128)}, u32[]{:S(2)}) copy-start(f32[3,1024,256]{2,1,0:T(8,128)} %subtract_subtract_fusion) | copy-start | bytes 9437188
  378.6 6.9 %copy-start.3 = (f32[1024,1024]{1,0:T(8,128)S(1)}, f32[1024,1024]{1,0:T(8,128)}, u32[]{:S(2)}) copy-start(f32[1024,1024]{1,0:T(8,128)} %fusion.44) | copy-start | bytes 12582916
Sparse Core Ops, SparseCore 0:
  416.4 152.1 reduce-scatter.1
where the time goes:
time: 584 us; the launch traced here: 578 us
  waiting for transfers between devices  396 us (68%)
  matrix products  62.4 us (11%)
  local copies, waits for them, and re-layouts  53.6 us (9%)
  starting transfers between devices  27.5 us (5%)
  other arithmetic  24.4 us (4%)
  between operations  13.9 us (2%)
    all_to_all x2, waiting for transfers between devices, by_batch(): lax.all_to_all(piece, ('idx', 'half'), split_axis=0, concat_axis=0, tiled...  235 us
    reduce_scatter x1, waiting for transfers between devices, on_device(): lax.psum_scatter(form(left_local, right_local, norm_scale), ('idx', 'half...  152 us
    transpose x4, local copies, waits for them, and re-layouts, by_batch(): piece = blocks[:, :, start:start + size].transpose(1, 0, 2, 3, 4)  28.4 us
    all_to_all x2, starting transfers between devices, by_batch(): lax.all_to_all(piece, ('idx', 'half'), split_axis=0, concat_axis=0, tiled...  27.1 us
    dot_general x6, matrix products, complex_product(): jnp.einsum(pattern, left_real + left_imag, right_real + right_imag, preci...  23.6 us
    dot_general x6, matrix products, complex_product(): first_term = jnp.einsum(pattern, left_real, right_real, precision=HIGH)  20.8 us
    dot_general x6, matrix products, complex_product(): second_term = jnp.einsum(pattern, left_imag, right_imag, precision=HIGH)  18 us
    transpose x2, local copies, waits for them, and re-layouts, by_batch(): got.transpose(1, 2, 3, 0, 4, 5)  14.3 us
  transfers between devices with their start and end apart: 4, of which 4 were waited for; matrix products, arithmetic and copies ran while one was open for 10% of the time, Pallas kernels for 0%

commit v1 on v0

--- a/solution.py
+++ b/solution.py
@@ -6,6 +6,22 @@
 
 HIGH = lax.Precision.HIGH
 CHUNKS = (3, 1)
+
+
+def exchange_in_pairs(array, axis, split, join):
+    ways, here = (lax.axis_size(axis), lax.axis_index(axis))
+    width = array.shape[split] // ways
+    lengths = list(array.shape)
+    lengths[split] = width
+    height = lengths[join]
+    lengths[join] = height * ways
+    full = jnp.zeros(lengths, array.dtype)
+    for mask in range(ways):
+        part = lax.dynamic_slice_in_dim(array, (here ^ mask) * width, width, axis=split)
+        if mask:
+            part = lax.ppermute(part, axis, [(d, d ^ mask) for d in range(ways)])
+        full = lax.dynamic_update_slice_in_dim(full, part, (here ^ mask) * height, axis=join)
+    return full
 
 
 def swapped(x, axis, bit):
@@ -49,9 +65,7 @@
     start = 0
     for size in sizes:
         piece = blocks[:, :, start : start + size].transpose(1, 0, 2, 3, 4)
-        received.append(
-            lax.all_to_all(piece, ("idx", "half"), split_axis=0, concat_axis=0, tiled=True)
-        )
+        received.append(exchange_in_pairs(piece, ("idx", "half"), 0, 0))
         start += size
     outgoing = lax.dynamic_slice_in_dim(left_local, (1 - half_index) * mine, mine, 1)
     own = lax.dynamic_slice_in_dim(left_local, half_index * mine, mine, 1)

time: 584 us -> 695 us (1.19)
  starting transfers between devices: 27.5 us -> 148 us
  waiting for transfers between devices: 396 us -> 341 us
  local copies, waits for them, and re-layouts: 53.6 us -> 94.5 us
    all_to_all x2 -> x0, waiting for transfers between devices: 235 us -> none  [by_batch(): lax.all_to_all(piece, ('idx', 'half'), split_axis=0, concat_axis=0, tiled...]
    ppermute x0 -> x30, waiting for transfers between devices: none -> 177 us  [exchange_in_pairs(): part = lax.ppermute(part, axis, [(d, d ^ mask) for d in range(ways)])]
    ppermute x0 -> x30, starting transfers between devices: none -> 148 us  [exchange_in_pairs(): part = lax.ppermute(part, axis, [(d, d ^ mask) for d in range(ways)])]
    dynamic_update_slice x0 -> x32, local copies, waits for them, and re-layouts: none -> 32.9 us  [exchange_in_pairs(): lax.dynamic_update_slice_in_dim(full, part, (here ^ mask) * height, axis=...]
    transpose x4 -> x0, local copies, waits for them, and re-layouts: 28.4 us -> none  [by_batch(): piece = blocks[:, :, start:start + size].transpose(1, 0, 2, 3, 4)]
    all_to_all x2 -> x0, starting transfers between devices: 27.1 us -> none  [by_batch(): lax.all_to_all(piece, ('idx', 'half'), split_axis=0, concat_axis=0, tiled...]
    slice x0 -> x2, local copies, waits for them, and re-layouts: none -> 16.7 us  [by_batch(): piece = blocks[:, :, start:start + size].transpose(1, 0, 2, 3, 4)]
    dynamic_slice x0 -> x2, local copies, waits for them, and re-layouts: none -> 12.2 us  [exchange_in_pairs(): lax.dynamic_slice_in_dim(array, (here ^ mask) * width, width, axis=split)]
  transfers between devices with their start and end apart: 4 -> 32, of which waited for: 4 -> 13; matrix products, arithmetic and copies ran while one was open for 10% -> 14% of each run, Pallas kernels for 0% -> 0%
where the time goes in v1:
time: 695 us; the launch traced here: 686 us
  waiting for transfers between devices  341 us (49%)
  starting transfers between devices  148 us (21%)
  local copies, waits for them, and re-layouts  94.5 us (14%)
  matrix products  60.5 us (9%)
  other arithmetic  27.5 us (4%)
  between operations  14.2 us (2%)
    ppermute x30, waiting for transfers between devices, exchange_in_pairs(): part = lax.ppermute(part, axis, [(d, d ^ mask) for d in range(ways)])  177 us
    reduce_scatter x1, waiting for transfers between devices, on_device(): lax.psum_scatter(form(left_local, right_local, norm_scale), ('idx', 'half...  164 us
    ppermute x30, starting transfers between devices, exchange_in_pairs(): part = lax.ppermute(part, axis, [(d, d ^ mask) for d in range(ways)])  148 us
    dynamic_update_slice x32, local copies, waits for them, and re-layouts, exchange_in_pairs(): lax.dynamic_update_slice_in_dim(full, part, (here ^ mask) * height, axis=...  32.9 us
    dot_general x6, matrix products, complex_product(): jnp.einsum(pattern, left_real + left_imag, right_real + right_imag, preci...  23.9 us
    dot_general x6, matrix products, complex_product(): first_term = jnp.einsum(pattern, left_real, right_real, precision=HIGH)  18.8 us
    dot_general x6, matrix products, complex_product(): second_term = jnp.einsum(pattern, left_imag, right_imag, precision=HIGH)  17.8 us
    slice x2, local copies, waits for them, and re-layouts, by_batch(): piece = blocks[:, :, start:start + size].transpose(1, 0, 2, 3, 4)  16.7 us
  transfers between devices with their start and end apart: 32, of which 13 were waited for; matrix products, arithmetic and copies ran while one was open for 14% of the time, Pallas kernels for 0%

profile of v1, /device:TPU:0, one launch (start us, length us, event | category | flops | bytes accessed | tf_op | source)
XLA Modules:
  0.0 685.9 jit_solution(4111905878539965840)
XLA Ops:
  6.5 7.2 %dynamic-slice_bitcast_fusion = f32[2,4,1024,256]{3,2,1,0:T(8,128)} fusion(f32[1,2,8,1024,256]{4,3,2,1,0:T(8,128)} %param.2, s32[]{:T(128)S(6)} %select_n.48), kind=kLoop, calls=%fused_computation.3 | loop fusion | bytes 16777220 | tf_op jit(solution)/shard_map/dynamic_slice | solution.py:70
  14.2 4.8 slice.94
  27.5 11.9 %slice.85 = f32[2,16,3,32,1024]{4,3,2,1,0:T(8,128)} slice(f32[2,16,4,32,1024]{4,3,2,1,0:T(8,128)} %bitcast.285), slice={[0:2], [0:16], [0:3], [0:32], [0:1024]} | slice | bytes 25165824 | tf_op jit(solution)/shard_map/slice | solution.py:67
  39.4 8.2 %dynamic-slice_bitcast_fusion.1 = (f32[1,2,3,32,1024]{4,3,2,1,0:T(8,128)S(1)}, f32[1,2,3,32,1024]{4,3,2,1,0:T(8,128)S(1)}, f32[1,2,3,32,1024]{4,3,2,1,0:T(8,128)...) fusion(f32[2,16,3,32,1024]{4,3,2,1,0:T(8,128)} %slice.85, ...), kind=kLoop, calls=%fused_computation.84 | loop fusion | bytes 23593020 | tf_op jit(solution)/shard_map/dynamic_slice | solution.py:20
  47.6 6.2 broadcast_in_dim.6
  72.7 14.6 %collective-permute-done.21 = f32[1,2,1,32,1024]{4,3,1,0,2:T(8,128)S(1)} collective-permute-done((f32[1,2,1,32,1024]{4,3,1,0,2:T(8,128)}, f32[1,2,1,32,1024]{4,3,1,0,2:T(8,128)S(1)}, u32[]{:S(2)}, u32[]{:S(2)}) %collective-permute-start.21) | collective-permute-done | bytes 262176 | tf_op jit(solution)/shard_map/ppermute | solution.py:22
  94.8 18.6 %collective-permute-start.28 = (f32[1,2,1,32,1024]{4,3,1,0,2:T(8,128)}, f32[1,2,1,32,1024]{4,3,1,0,2:T(8,128)S(1)}, u32[]{:S(2)}, u32[]{:S(2)}) collective-permute-start(f32[1,2,1,32,1024]{4,3,1,0,2:T(8,128)} %get-tuple-element.24), channel_id=1, source_target_pairs={{0,13},{1,12},{2,15},{3,14},{4,9},{5,8},{6,11},{7,10},{8,5},{9,4},... | collective-permute-start | bytes 786440 | tf_op jit(solution)/shard_map/ppermute | solution.py:22
  113.4 9.1 %collective-permute-done.25 = f32[1,2,1,32,1024]{4,3,1,0,2:T(8,128)S(1)} collective-permute-done((f32[1,2,1,32,1024]{4,3,1,0,2:T(8,128)}, f32[1,2,1,32,1024]{4,3,1,0,2:T(8,128)S(1)}, u32[]{:S(2)}, u32[]{:S(2)}) %collective-permute-start.25) | collective-permute-done | bytes 262176 | tf_op jit(solution)/shard_map/ppermute | solution.py:22
  128.2 6.1 collective-permute-start.2
  135.8 4.6 collective-permute-start.30
  142.5 4.6 collective-permute-done.30
  147.2 19.1 %collective-permute-start.4 = (f32[1,2,3,32,1024]{4,3,2,1,0:T(8,128)S(1)}, f32[1,2,3,32,1024]{4,3,2,1,0:T(8,128)S(1)}, u32[]{:S(2)}, u32[]{:S(2)}) collective-permute-start(f32[1,2,3,32,1024]{4,3,2,1,0:T(8,128)S(1)} %copy-done.9), channel_id=1, source_target_pairs={{0,4},{1,5},{2,6},{3,7},{4,0},{5,1},{6,2},{7,3},{8,12},{9,13},{10,... | collective-permute-start | bytes 2359304 | tf_op jit(solution)/shard_map/ppermute | solution.py:22
  174.0 13.3 %collective-permute-start.7 = (f32[1,2,3,32,1024]{4,3,2,1,0:T(8,128)S(1)}, f32[1,2,3,32,1024]{4,3,2,1,0:T(8,128)S(1)}, u32[]{:S(2)}, u32[]{:S(2)}) collective-permute-start(f32[1,2,3,32,1024]{4,3,2,1,0:T(8,128)S(1)} %copy-done.6), channel_id=1, source_target_pairs={{0,7},{1,6},{2,5},{3,4},{4,3},{5,2},{6,1},{7,0},{8,15},{9,14},{10,... | collective-permute-start | bytes 2359304 | tf_op jit(solution)/shard_map/ppermute | solution.py:22
  189.4 27.6 %collective-permute-done.5 = f32[1,2,3,32,1024]{4,3,2,1,0:T(8,128)S(1)} collective-permute-done((f32[1,2,3,32,1024]{4,3,2,1,0:T(8,128)S(1)}, f32[1,2,3,32,1024]{4,3,2,1,0:T(8,128)S(1)}, u32[]{:S(2)}, u32[]{:S(2)}) %collective-permute-start.5) | collective-permute-done | bytes 786464 | tf_op jit(solution)/shard_map/ppermute | solution.py:22
  219.4 32.4 %collective-permute-done.6 = f32[1,2,3,32,1024]{4,3,2,1,0:T(8,128)S(1)} collective-permute-done((f32[1,2,3,32,1024]{4,3,2,1,0:T(8,128)S(1)}, f32[1,2,3,32,1024]{4,3,2,1,0:T(8,128)S(1)}, u32[]{:S(2)}, u32[]{:S(2)}) %collective-permute-start.6) | collective-permute-done | bytes 786464 | tf_op jit(solution)/shard_map/ppermute | solution.py:22
  252.7 14.7 %collective-permute-done.7 = f32[1,2,3,32,1024]{4,3,2,1,0:T(8,128)S(1)} collective-permute-done((f32[1,2,3,32,1024]{4,3,2,1,0:T(8,128)S(1)}, f32[1,2,3,32,1024]{4,3,2,1,0:T(8,128)S(1)}, u32[]{:S(2)}, u32[]{:S(2)}) %collective-permute-start.7) | collective-permute-done | bytes 786464 | tf_op jit(solution)/shard_map/ppermute | solution.py:22
  272.9 54.0 %collective-permute-start.13 = (f32[1,2,3,32,1024]{4,3,2,1,0:T(8,128)S(1)}, f32[1,2,3,32,1024]{4,3,2,1,0:T(8,128)S(1)}, u32[]{:S(2)}, u32[]{:S(2)}) collective-permute-start(f32[1,2,3,32,1024]{4,3,2,1,0:T(8,128)S(1)} %get-tuple-element.9), channel_id=1, source_target_pairs={{0,13},{1,12},{2,15},{3,14},{4,9},{5,8},{6,11},{7,10},{8,5},{9,4},... | collective-permute-start | bytes 2359304 | tf_op jit(solution)/shard_map/ppermute | solution.py:22
  327.9 28.6 %collective-permute-done.10 = f32[1,2,3,32,1024]{4,3,2,1,0:T(8,128)S(1)} collective-permute-done((f32[1,2,3,32,1024]{4,3,2,1,0:T(8,128)S(1)}, f32[1,2,3,32,1024]{4,3,2,1,0:T(8,128)S(1)}, u32[]{:S(2)}, u32[]{:S(2)}) %collective-permute-start.10) | collective-permute-done | bytes 786464 | tf_op jit(solution)/shard_map/ppermute | solution.py:22
  356.5 5.3 collective-permute-start.14
  362.7 26.6 %collective-permute-done.11 = f32[1,2,3,32,1024]{4,3,2,1,0:T(8,128)S(1)} collective-permute-done((f32[1,2,3,32,1024]{4,3,2,1,0:T(8,128)S(1)}, f32[1,2,3,32,1024]{4,3,2,1,0:T(8,128)S(1)}, u32[]{:S(2)}, u32[]{:S(2)}) %collective-permute-start.11) | collective-permute-done | bytes 786464 | tf_op jit(solution)/shard_map/ppermute | solution.py:22
  389.3 5.6 collective-permute-start.15
  400.6 12.2 %collective-permute-done.15 = f32[1,2,3,32,1024]{4,3,2,1,0:T(8,128)S(1)} collective-permute-done((f32[1,2,3,32,1024]{4,3,2,1,0:T(8,128)S(1)}, f32[1,2,3,32,1024]{4,3,2,1,0:T(8,128)S(1)}, u32[]{:S(2)}, u32[]{:S(2)}) %collective-permute-start.15) | collective-permute-done | bytes 786464 | tf_op jit(solution)/shard_map/ppermute | solution.py:22
  413.8 12.0 %copy.8 = f32[2,2,3,8,32,1024]{5,4,3,2,1,0:T(8,128)} copy(f32[2,2,3,8,32,1024]{5,4,2,1,0,3:T(8,128)} %bitcast.21) | data formatting | bytes 25165824 | tf_op jit(solution)/shard_map/transpose | solution.py:80
  425.9 4.6 fusion.15
  430.4 5.1 fusion.14
  437.4 10.0 %bitcast_select_fusion = (f32[2,4,1024,256]{3,2,1,0:T(8,128)}, f32[2,4,1024,256]{3,2,1,0:T(8,128)S(1)}) fusion(f32[2,4,1024,256]{3,2,1,0:T(8,128)} %collective-permute-done, f32[1,2,8,1024,256]{4,3,2,1,0:T(8,128)} %param.2, s32[]{:T(128)S(6)} %select_n.47, pred[]{:T(512)S(6)} %eq.3), kind=kLoop, calls=%fused_computation.1 | loop fusion | flops 4194304 | bytes 33554436 | tf_op jit(solution)/shard_map/jit(_where)/select_n | solution.py:75
  454.5 9.0 %fusion.17 = f32[1024,1024,1]{1,0,2:T(8,128)} fusion(f32[2,4,1024,256]{3,2,1,0:T(8,128)} %get-tuple-element.5, f32[3,1024,256]{2,1,0:T(8,128)S(1)} %fusion.13, f32[3,1024,256]{2,1,0:T(8,128)S(1)} %fusion.16), kind=kOutput, calls=%fused_computation.32 | convolution fusion | flops 4832624640 | bytes 13631488 | tf_op jit(solution)/shard_map/bml,bol->mo/dot_general | solution.py:32
  474.4 6.8 fusion.18
  481.1 8.7 %fusion.4 = f32[1024,1,1024]{2,0,1:T(8,128)} fusion(f32[1024,1024,1]{1,0,2:T(8,128)} %fusion.18, f32[1024,1024,1]{1,0,2:T(8,128)} %fusion.17, f32[1024,1024]{1,0:T(8,128)S(1)} %fusion.44, f32[1024,1024]{1,0:T(8,128)} %fusion.41), kind=kLoop, calls=%fused_computation.10 | loop fusion | flops 3145728 | bytes 20971520 | tf_op jit(solution)/shard_map/stack | solution.py:88
  489.8 13.5 %fusion.2 = f32[1024,1,1024]{2,0,1:T(8,128)} fusion(f32[1024,1024,1]{1,0,2:T(8,128)} %fusion.18, f32[1024,1024,1]{1,0,2:T(8,128)} %fusion.17, f32[1024,1024]{1,0:T(8,128)} %fusion.41, f32[1024,1024]{1,0:T(8,128)} %fusion.39, f32[1024,1024]{1,0:T(8,128)S(1)} %fusion.44, f32[2,4,1024,256]{3,2,1,0:T(8,128)} %get-tuple-element.5, ...), kind=kOutput, calls=%fused_computation.7 | convolution fusion | flops 4839440384 | bytes 40894464 | tf_op jit(solution)/shard_map/bml,bol->mo/dot_general | solution.py:34
  503.4 8.8 %maximum_multiply_fusion = f32[1024,2,1024]{2,0,1:T(8,128)} fusion(f32[1024,1,1024]{2,0,1:T(8,128)} %fusion.2, f32[1024,1,1024]{2,0,1:T(8,128)} %fusion.4), kind=kLoop, calls=%fused_computation | loop fusion | flops 4194304 | bytes 16777216 | tf_op jit(solution)/shard_map/mul | solution.py:88
  512.2 164.2 %reduce-scatter.2.cloned.1.call-done = f32[64,2,1024]{2,0,1:T(8,128)} async-done(((f32[1024,2,1024]{2,0,1:T(8,128)}), f32[64,2,1024]{2,0,1:T(8,128)}) %reduce-scatter.2.cloned.1.call-update) | async-done | bytes 524304 | tf_op jit(solution)/shard_map/reduce_scatter | solution.py:98
  (127 shorter events, 93.7 us)
Async XLA Ops:
  6.5 669.8 %reduce-scatter.2.cloned.1.call-start = ((), (), s32[]{:S(2)}) async-start(), calls=%async_computation.1 | async-start | bytes 8912896 | tf_op jit(solution)/shard_map/reduce_scatter | solution.py:98
  13.7 423.7 %collective-permute-start = (f32[2,4,1024,256]{3,2,1,0:T(8,128)}, f32[2,4,1024,256]{3,2,1,0:T(8,128)}, u32[]{:S(2)}, u32[]{:S(2)}) collective-permute-start(f32[2,4,1024,256]{3,2,1,0:T(8,128)} %dynamic-slice_bitcast_fusion), channel_id=1, source_target_pairs={{0,1},{1,0},{2,3},{3,2},{4,5},{5,4},{6,7},{7,6},{8,9},{9,8},{10,11... | collective-permute-start | bytes 25165832 | tf_op jit(solution)/shard_map/ppermute | solution.py:28
  22.9 37.2 %collective-permute-start.16 = (f32[1,2,1,32,1024]{4,3,1,0,2:T(8,128)}, f32[1,2,1,32,1024]{4,3,1,0,2:T(8,128)}, u32[]{:S(2)}, u32[]{:S(2)}) collective-permute-start(f32[1,2,1,32,1024]{4,3,1,0,2:T(8,128)} %get-tuple-element.36), channel_id=1, source_target_pairs={{0,1},{1,0},{2,3},{3,2},{4,5},{5,4},{6,7},{7,6},{8,9},{9,8},{10,11... | collective-permute-start | bytes 786440 | tf_op jit(solution)/shard_map/ppermute | solution.py:22
  23.0 39.3 %collective-permute-start.17 = (f32[1,2,1,32,1024]{4,3,1,0,2:T(8,128)}, f32[1,2,1,32,1024]{4,3,1,0,2:T(8,128)}, u32[]{:S(2)}, u32[]{:S(2)}) collective-permute-start(f32[1,2,1,32,1024]{4,3,1,0,2:T(8,128)} %get-tuple-element.35), channel_id=1, source_target_pairs={{0,2},{1,3},{2,0},{3,1},{4,6},{5,7},{6,4},{7,5},{8,10},{9,11},{10,... | collective-permute-start | bytes 786440 | tf_op jit(solution)/shard_map/ppermute | solution.py:22
  25.9 40.5 %collective-permute-start.18 = (f32[1,2,1,32,1024]{4,3,1,0,2:T(8,128)}, f32[1,2,1,32,1024]{4,3,1,0,2:T(8,128)}, u32[]{:S(2)}, u32[]{:S(2)}) collective-permute-start(f32[1,2,1,32,1024]{4,3,1,0,2:T(8,128)} %get-tuple-element.34), channel_id=1, source_target_pairs={{0,3},{1,2},{2,1},{3,0},{4,7},{5,6},{6,5},{7,4},{8,11},{9,10},{10,... | collective-permute-start | bytes 786440 | tf_op jit(solution)/shard_map/ppermute | solution.py:22
  25.9 40.5 %collective-permute-start.19 = (f32[1,2,1,32,1024]{4,3,1,0,2:T(8,128)}, f32[1,2,1,32,1024]{4,3,1,0,2:T(8,128)}, u32[]{:S(2)}, u32[]{:S(2)}) collective-permute-start(f32[1,2,1,32,1024]{4,3,1,0,2:T(8,128)} %get-tuple-element.33), channel_id=1, source_target_pairs={{0,4},{1,5},{2,6},{3,7},{4,0},{5,1},{6,2},{7,3},{8,12},{9,13},{10,... | collective-permute-start | bytes 786440 | tf_op jit(solution)/shard_map/ppermute | solution.py:22
  60.1 12.4 %collective-permute-start.20 = (f32[1,2,1,32,1024]{4,3,1,0,2:T(8,128)}, f32[1,2,1,32,1024]{4,3,1,0,2:T(8,128)S(1)}, u32[]{:S(2)}, u32[]{:S(2)}) collective-permute-start(f32[1,2,1,32,1024]{4,3,1,0,2:T(8,128)} %get-tuple-element.32), channel_id=1, source_target_pairs={{0,5},{1,4},{2,7},{3,6},{4,1},{5,0},{6,3},{7,2},{8,13},{9,12},{10,... | collective-permute-start | bytes 786440 | tf_op jit(solution)/shard_map/ppermute | solution.py:22
  62.3 25.0 %collective-permute-start.21 = (f32[1,2,1,32,1024]{4,3,1,0,2:T(8,128)}, f32[1,2,1,32,1024]{4,3,1,0,2:T(8,128)S(1)}, u32[]{:S(2)}, u32[]{:S(2)}) collective-permute-start(f32[1,2,1,32,1024]{4,3,1,0,2:T(8,128)} %get-tuple-element.31), channel_id=1, source_target_pairs={{0,6},{1,7},{2,4},{3,5},{4,2},{5,3},{6,0},{7,1},{8,14},{9,15},{10,... | collective-permute-start | bytes 786440 | tf_op jit(solution)/shard_map/ppermute | solution.py:22
  66.4 25.3 %collective-permute-start.22 = (f32[1,2,1,32,1024]{4,3,1,0,2:T(8,128)}, f32[1,2,1,32,1024]{4,3,1,0,2:T(8,128)S(1)}, u32[]{:S(2)}, u32[]{:S(2)}) collective-permute-start(f32[1,2,1,32,1024]{4,3,1,0,2:T(8,128)} %get-tuple-element.30), channel_id=1, source_target_pairs={{0,7},{1,6},{2,5},{3,4},{4,3},{5,2},{6,1},{7,0},{8,15},{9,14},{10,... | collective-permute-start | bytes 786440 | tf_op jit(solution)/shard_map/ppermute | solution.py:22
  66.5 25.3 %collective-permute-start.23 = (f32[1,2,1,32,1024]{4,3,1,0,2:T(8,128)}, f32[1,2,1,32,1024]{4,3,1,0,2:T(8,128)S(1)}, u32[]{:S(2)}, u32[]{:S(2)}) collective-permute-start(f32[1,2,1,32,1024]{4,3,1,0,2:T(8,128)} %get-tuple-element.29), channel_id=1, source_target_pairs={{0,8},{1,9},{2,10},{3,11},{4,12},{5,13},{6,14},{7,15},{8,0},{9,1},... | collective-permute-start | bytes 786440 | tf_op jit(solution)/shard_map/ppermute | solution.py:22
  72.5 22.3 %collective-permute-start.24 = (f32[1,2,1,32,1024]{4,3,1,0,2:T(8,128)}, f32[1,2,1,32,1024]{4,3,1,0,2:T(8,128)S(1)}, u32[]{:S(2)}, u32[]{:S(2)}) collective-permute-start(f32[1,2,1,32,1024]{4,3,1,0,2:T(8,128)} %get-tuple-element.28), channel_id=1, source_target_pairs={{0,9},{1,8},{2,11},{3,10},{4,13},{5,12},{6,15},{7,14},{8,1},{9,0},... | collective-permute-start | bytes 786440 | tf_op jit(solution)/shard_map/ppermute | solution.py:22
  87.3 35.2 %collective-permute-start.25 = (f32[1,2,1,32,1024]{4,3,1,0,2:T(8,128)}, f32[1,2,1,32,1024]{4,3,1,0,2:T(8,128)S(1)}, u32[]{:S(2)}, u32[]{:S(2)}) collective-permute-start(f32[1,2,1,32,1024]{4,3,1,0,2:T(8,128)} %get-tuple-element.27), channel_id=1, source_target_pairs={{0,10},{1,11},{2,8},{3,9},{4,14},{5,15},{6,12},{7,13},{8,2},{9,3},... | collective-permute-start | bytes 786440 | tf_op jit(solution)/shard_map/ppermute | solution.py:22
  91.8 36.3 %collective-permute-start.26 = (f32[1,2,1,32,1024]{4,3,1,0,2:T(8,128)}, f32[1,2,1,32,1024]{4,3,1,0,2:T(8,128)S(1)}, u32[]{:S(2)}, u32[]{:S(2)}) collective-permute-start(f32[1,2,1,32,1024]{4,3,1,0,2:T(8,128)} %get-tuple-element.26), channel_id=1, source_target_pairs={{0,11},{1,10},{2,9},{3,8},{4,15},{5,14},{6,13},{7,12},{8,3},{9,2},... | collective-permute-start | bytes 786440 | tf_op jit(solution)/shard_map/ppermute | solution.py:22
  91.8 36.4 %collective-permute-start.27 = (f32[1,2,1,32,1024]{4,3,1,0,2:T(8,128)}, f32[1,2,1,32,1024]{4,3,1,0,2:T(8,128)S(1)}, u32[]{:S(2)}, u32[]{:S(2)}) collective-permute-start(f32[1,2,1,32,1024]{4,3,1,0,2:T(8,128)} %get-tuple-element.25), channel_id=1, source_target_pairs={{0,12},{1,13},{2,14},{3,15},{4,8},{5,9},{6,10},{7,11},{8,4},{9,5},... | collective-permute-start | bytes 786440 | tf_op jit(solution)/shard_map/ppermute | solution.py:22
  94.8 41.0 %collective-permute-start.28 = (f32[1,2,1,32,1024]{4,3,1,0,2:T(8,128)}, f32[1,2,1,32,1024]{4,3,1,0,2:T(8,128)S(1)}, u32[]{:S(2)}, u32[]{:S(2)}) collective-permute-start(f32[1,2,1,32,1024]{4,3,1,0,2:T(8,128)} %get-tuple-element.24), channel_id=1, source_target_pairs={{0,13},{1,12},{2,15},{3,14},{4,9},{5,8},{6,11},{7,10},{8,5},{9,4},... | collective-permute-start | bytes 786440 | tf_op jit(solution)/shard_map/ppermute | solution.py:22
  122.5 13.3 %collective-permute-start.29 = (f32[1,2,1,32,1024]{4,3,1,0,2:T(8,128)}, f32[1,2,1,32,1024]{4,3,1,0,2:T(8,128)S(1)}, u32[]{:S(2)}, u32[]{:S(2)}) collective-permute-start(f32[1,2,1,32,1024]{4,3,1,0,2:T(8,128)} %get-tuple-element.23), channel_id=1, source_target_pairs={{0,14},{1,15},{2,12},{3,13},{4,10},{5,11},{6,8},{7,9},{8,6},{9,7},... | collective-permute-start | bytes 786440 | tf_op jit(solution)/shard_map/ppermute | solution.py:22
  128.1 42.3 %collective-permute-start.1 = (f32[1,2,3,32,1024]{4,3,2,1,0:T(8,128)S(1)}, f32[1,2,3,32,1024]{4,3,2,1,0:T(8,128)S(1)}, u32[]{:S(2)}, u32[]{:S(2)}) collective-permute-start(f32[1,2,3,32,1024]{4,3,2,1,0:T(8,128)S(1)} %copy-done.12), channel_id=1, source_target_pairs={{0,1},{1,0},{2,3},{3,2},{4,5},{5,4},{6,7},{7,6},{8,9},{9,8},{10,11... | collective-permute-start | bytes 2359304 | tf_op jit(solution)/shard_map/ppermute | solution.py:22
  128.2 42.3 %collective-permute-start.2 = (f32[1,2,3,32,1024]{4,3,2,1,0:T(8,128)S(1)}, f32[1,2,3,32,1024]{4,3,2,1,0:T(8,128)S(1)}, u32[]{:S(2)}, u32[]{:S(2)}) collective-permute-start(f32[1,2,3,32,1024]{4,3,2,1,0:T(8,128)S(1)} %copy-done.11), channel_id=1, source_target_pairs={{0,2},{1,3},{2,0},{3,1},{4,6},{5,7},{6,4},{7,5},{8,10},{9,11},{10,... | collective-permute-start | bytes 2359304 | tf_op jit(solution)/shard_map/ppermute | solution.py:22
  135.8 38.2 %collective-permute-start.3 = (f32[1,2,3,32,1024]{4,3,2,1,0:T(8,128)S(1)}, f32[1,2,3,32,1024]{4,3,2,1,0:T(8,128)S(1)}, u32[]{:S(2)}, u32[]{:S(2)}) collective-permute-start(f32[1,2,3,32,1024]{4,3,2,1,0:T(8,128)S(1)} %copy-done.10), channel_id=1, source_target_pairs={{0,3},{1,2},{2,1},{3,0},{4,7},{5,6},{6,5},{7,4},{8,11},{9,10},{10,... | collective-permute-start | bytes 2359304 | tf_op jit(solution)/shard_map/ppermute | solution.py:22
  135.8 11.4 %collective-permute-start.30 = (f32[1,2,1,32,1024]{4,3,1,0,2:T(8,128)S(1)}, f32[1,2,1,32,1024]{4,3,1,0,2:T(8,128)S(1)}, u32[]{:S(2)}, u32[]{:S(2)}) collective-permute-start(f32[1,2,1,32,1024]{4,3,1,0,2:T(8,128)S(1)} %get-tuple-element.22), channel_id=1, source_target_pairs={{0,15},{1,14},{2,13},{3,12},{4,11},{5,10},{6,9},{7,8},{8,7},{9,6},... | collective-permute-start | bytes 786440 | tf_op jit(solution)/shard_map/ppermute | solution.py:22
  147.2 40.7 %collective-permute-start.4 = (f32[1,2,3,32,1024]{4,3,2,1,0:T(8,128)S(1)}, f32[1,2,3,32,1024]{4,3,2,1,0:T(8,128)S(1)}, u32[]{:S(2)}, u32[]{:S(2)}) collective-permute-start(f32[1,2,3,32,1024]{4,3,2,1,0:T(8,128)S(1)} %copy-done.9), channel_id=1, source_target_pairs={{0,4},{1,5},{2,6},{3,7},{4,0},{5,1},{6,2},{7,3},{8,12},{9,13},{10,... | collective-permute-start | bytes 2359304 | tf_op jit(solution)/shard_map/ppermute | solution.py:22
  170.4 46.7 %collective-permute-start.5 = (f32[1,2,3,32,1024]{4,3,2,1,0:T(8,128)S(1)}, f32[1,2,3,32,1024]{4,3,2,1,0:T(8,128)S(1)}, u32[]{:S(2)}, u32[]{:S(2)}) collective-permute-start(f32[1,2,3,32,1024]{4,3,2,1,0:T(8,128)S(1)} %copy-done.8), channel_id=1, source_target_pairs={{0,5},{1,4},{2,7},{3,6},{4,1},{5,0},{6,3},{7,2},{8,13},{9,12},{10,... | collective-permute-start | bytes 2359304 | tf_op jit(solution)/shard_map/ppermute | solution.py:22
  170.5 81.2 %collective-permute-start.6 = (f32[1,2,3,32,1024]{4,3,2,1,0:T(8,128)S(1)}, f32[1,2,3,32,1024]{4,3,2,1,0:T(8,128)S(1)}, u32[]{:S(2)}, u32[]{:S(2)}) collective-permute-start(f32[1,2,3,32,1024]{4,3,2,1,0:T(8,128)S(1)} %copy-done.7), channel_id=1, source_target_pairs={{0,6},{1,7},{2,4},{3,5},{4,2},{5,3},{6,0},{7,1},{8,14},{9,15},{10,... | collective-permute-start | bytes 2359304 | tf_op jit(solution)/shard_map/ppermute | solution.py:22
  174.0 93.5 %collective-permute-start.7 = (f32[1,2,3,32,1024]{4,3,2,1,0:T(8,128)S(1)}, f32[1,2,3,32,1024]{4,3,2,1,0:T(8,128)S(1)}, u32[]{:S(2)}, u32[]{:S(2)}) collective-permute-start(f32[1,2,3,32,1024]{4,3,2,1,0:T(8,128)S(1)} %copy-done.6), channel_id=1, source_target_pairs={{0,7},{1,6},{2,5},{3,4},{4,3},{5,2},{6,1},{7,0},{8,15},{9,14},{10,... | collective-permute-start | bytes 2359304 | tf_op jit(solution)/shard_map/ppermute | solution.py:22
  187.9 82.4 %collective-permute-start.8 = (f32[1,2,3,32,1024]{4,3,2,1,0:T(8,128)S(1)}, f32[1,2,3,32,1024]{4,3,2,1,0:T(8,128)S(1)}, u32[]{:S(2)}, u32[]{:S(2)}) collective-permute-start(f32[1,2,3,32,1024]{4,3,2,1,0:T(8,128)S(1)} %copy-done.5), channel_id=1, source_target_pairs={{0,8},{1,9},{2,10},{3,11},{4,12},{5,13},{6,14},{7,15},{8,0},{9,1},... | collective-permute-start | bytes 2359304 | tf_op jit(solution)/shard_map/ppermute | solution.py:22
  217.1 55.8 %collective-permute-start.9 = (f32[1,2,3,32,1024]{4,3,2,1,0:T(8,128)S(1)}, f32[1,2,3,32,1024]{4,3,2,1,0:T(8,128)S(1)}, u32[]{:S(2)}, u32[]{:S(2)}) collective-permute-start(f32[1,2,3,32,1024]{4,3,2,1,0:T(8,128)S(1)} %copy-done.4), channel_id=1, source_target_pairs={{0,9},{1,8},{2,11},{3,10},{4,13},{5,12},{6,15},{7,14},{8,1},{9,0},... | collective-permute-start | bytes 2359304 | tf_op jit(solution)/shard_map/ppermute | solution.py:22
  251.7 104.8 %collective-permute-start.10 = (f32[1,2,3,32,1024]{4,3,2,1,0:T(8,128)S(1)}, f32[1,2,3,32,1024]{4,3,2,1,0:T(8,128)S(1)}, u32[]{:S(2)}, u32[]{:S(2)}) collective-permute-start(f32[1,2,3,32,1024]{4,3,2,1,0:T(8,128)S(1)} %copy-done.3), channel_id=1, source_target_pairs={{0,10},{1,11},{2,8},{3,9},{4,14},{5,15},{6,12},{7,13},{8,2},{9,3},... | collective-permute-start | bytes 2359304 | tf_op jit(solution)/shard_map/ppermute | solution.py:22
  267.4 121.9 %collective-permute-start.11 = (f32[1,2,3,32,1024]{4,3,2,1,0:T(8,128)S(1)}, f32[1,2,3,32,1024]{4,3,2,1,0:T(8,128)S(1)}, u32[]{:S(2)}, u32[]{:S(2)}) collective-permute-start(f32[1,2,3,32,1024]{4,3,2,1,0:T(8,128)S(1)} %copy-done.2), channel_id=1, source_target_pairs={{0,11},{1,10},{2,9},{3,8},{4,15},{5,14},{6,13},{7,12},{8,3},{9,2},... | collective-permute-start | bytes 2359304 | tf_op jit(solution)/shard_map/ppermute | solution.py:22
  270.3 127.5 %collective-permute-start.12 = (f32[1,2,3,32,1024]{4,3,2,1,0:T(8,128)S(1)}, f32[1,2,3,32,1024]{4,3,2,1,0:T(8,128)S(1)}, u32[]{:S(2)}, u32[]{:S(2)}) collective-permute-start(f32[1,2,3,32,1024]{4,3,2,1,0:T(8,128)S(1)} %get-tuple-element.10), channel_id=1, source_target_pairs={{0,12},{1,13},{2,14},{3,15},{4,8},{5,9},{6,10},{7,11},{8,4},{9,5},... | collective-permute-start | bytes 2359304 | tf_op jit(solution)/shard_map/ppermute | solution.py:22
  272.9 125.8 %collective-permute-start.13 = (f32[1,2,3,32,1024]{4,3,2,1,0:T(8,128)S(1)}, f32[1,2,3,32,1024]{4,3,2,1,0:T(8,128)S(1)}, u32[]{:S(2)}, u32[]{:S(2)}) collective-permute-start(f32[1,2,3,32,1024]{4,3,2,1,0:T(8,128)S(1)} %get-tuple-element.9), channel_id=1, source_target_pairs={{0,13},{1,12},{2,15},{3,14},{4,9},{5,8},{6,11},{7,10},{8,5},{9,4},... | collective-permute-start | bytes 2359304 | tf_op jit(solution)/shard_map/ppermute | solution.py:22
  356.5 43.2 %collective-permute-start.14 = (f32[1,2,3,32,1024]{4,3,2,1,0:T(8,128)S(1)}, f32[1,2,3,32,1024]{4,3,2,1,0:T(8,128)S(1)}, u32[]{:S(2)}, u32[]{:S(2)}) collective-permute-start(f32[1,2,3,32,1024]{4,3,2,1,0:T(8,128)S(1)} %get-tuple-element.8), channel_id=1, source_target_pairs={{0,14},{1,15},{2,12},{3,13},{4,10},{5,11},{6,8},{7,9},{8,6},{9,7},... | collective-permute-start | bytes 2359304 | tf_op jit(solution)/shard_map/ppermute | solution.py:22
  389.3 23.5 %collective-permute-start.15 = (f32[1,2,3,32,1024]{4,3,2,1,0:T(8,128)S(1)}, f32[1,2,3,32,1024]{4,3,2,1,0:T(8,128)S(1)}, u32[]{:S(2)}, u32[]{:S(2)}) collective-permute-start(f32[1,2,3,32,1024]{4,3,2,1,0:T(8,128)S(1)} %get-tuple-element.7), channel_id=1, source_target_pairs={{0,15},{1,14},{2,13},{3,12},{4,11},{5,10},{6,9},{7,8},{8,7},{9,6},... | collective-permute-start | bytes 2359304 | tf_op jit(solution)/shard_map/ppermute | solution.py:22
  (15 other events, 583.8 us)
Sparse Core Ops, SparseCore 0:
  512.3 164.0 reduce-scatter.1
